TPU v7x, 128 devices: a whole 4x4x4 slice. The times are simulated.
128 devices in a mesh: alpha: 64 (over z, y, x), beta: 2 (over core).
Axes of the slice: x: 4, y: 4, z: 4, core: 2. Of those that a mesh axis runs over, the one named last changes fastest.
Arguments:
- coeffs: bfloat16 [4096, 512], P('alpha', 'beta'), may hold values from -6 to 6
- integrals: bfloat16 [484, 484], replicated, may hold values from -0.0234375 to 0.0234375
- send_block: int32 [64, 512], P('alpha'), may hold values from 0 to 16, as said below
- alpha_slot: int32 [1024, 132], P('alpha'), may hold values from 0 to 255, as said below
- alpha_pair: int32 [1024, 132], P('alpha'), may hold values from 0 to 483, as said below
- alpha_parity: int32 [1024, 132], P('alpha'), may hold values from 0 to 1
- beta_pair: int32 [32, 132], P('beta'), may hold values from 0 to 483, as said below
- beta_target: int32 [32, 132], P('beta'), may hold values from 0 to 31
- beta_parity: int32 [32, 132], P('beta'), may hold values from 0 to 1
Outputs:
- sigma: float32 [4096, 512], P('alpha', 'beta')
Inputs may be any that keep to these rules, and one draw needn't show every extreme that they name: `send_block`: in each batch the filled slots from one sender to one receiver come first; at most 4 are filled, 4 is reached from every sender to some receiver in every batch, and some slots stay empty in every batch. `alpha_slot`: every entry names a slot that holds a block. `alpha_pair`: the pairs of one row are distinct. `beta_pair`: the pairs of one row are distinct.
All inputs are finite; a program needn't handle non-finite values.
Results may differ from a plain program's by a relative error of at most 0.0003.
Values may be sent and summed in bfloat16 or wider, within the bound.
A program may use at most 64 MiB of HBM per device.

v0:
```python
import jax
import jax.numpy as jnp
from jax import lax
from jax.sharding import PartitionSpec as P

P_SIZE = 484
EXC_BLK = 132
EXCB = 132
SB = 4
BBLK = 16
BATCHES = 2
CAP = 4


def block_sigma(received, entry_slot, entry_pair, entry_parity, integrals, pair_table, beta_blocks):
    slot_count = received.shape[0]
    factors = (1 - 2 * entry_parity).astype(jnp.float32)
    slot_hot = (
        (lax.broadcasted_iota(jnp.int32, (EXC_BLK, slot_count), 1) == entry_slot[:, None]).astype(
            jnp.float32
        )
        * factors[:, None]
    ).astype(jnp.bfloat16)
    signed = jnp.dot(slot_hot, received, preferred_element_type=jnp.float32).astype(jnp.bfloat16)
    pair_hot = (
        lax.broadcasted_iota(jnp.int32, (P_SIZE, EXC_BLK), 0) == entry_pair[None, :]
    ).astype(jnp.bfloat16)
    selected = jnp.dot(integrals, pair_hot, preferred_element_type=jnp.float32).astype(jnp.bfloat16)
    contracted = jnp.dot(selected, signed, preferred_element_type=jnp.float32)
    local_blocks = pair_table.shape[0]
    arranged = contracted.reshape(P_SIZE, SB, local_blocks, BBLK)
    summed = jnp.einsum("vup,psvb->sub", pair_table, arranged, precision=lax.Precision.HIGHEST)
    return summed.reshape(SB, beta_blocks * BBLK)


def on_device(
    coeffs,
    integrals,
    send_block,
    alpha_slot,
    alpha_pair,
    alpha_parity,
    beta_pair,
    beta_target,
    beta_parity,
):
    local_rows, local_columns = coeffs.shape
    local_blocks = local_rows // SB
    per_batch = local_blocks // BATCHES
    senders = lax.axis_size("alpha")
    slot_count = senders * CAP
    row_width = SB * local_columns
    beta_local = beta_pair.shape[0]
    beta_blocks = lax.axis_size("beta") * beta_local
    blocks = coeffs.reshape(local_blocks, row_width)
    padded = jnp.concatenate([blocks, jnp.zeros((1, row_width), jnp.bfloat16)], axis=0)
    send_lists = send_block.reshape(BATCHES, slot_count)
    beta_factor = (1 - 2 * beta_parity).astype(jnp.float32)
    target_hot = (
        lax.broadcasted_iota(jnp.int32, (beta_local, EXCB, beta_blocks), 2)
        == beta_target[:, :, None]
    ).astype(jnp.float32) * beta_factor[:, :, None]
    pair_onehot = (
        lax.broadcasted_iota(jnp.int32, (beta_local, EXCB, P_SIZE), 2) == beta_pair[:, :, None]
    ).astype(jnp.float32)
    pair_table = jnp.einsum(
        "veu,vep->vup", target_hot, pair_onehot, precision=lax.Precision.HIGHEST
    )
    outputs = []
    for batch_index in range(BATCHES):
        outgoing = padded[send_lists[batch_index]]
        received = lax.all_to_all(outgoing, "alpha", split_axis=0, concat_axis=0, tiled=True)
        first_block = batch_index * per_batch
        entries = (
            alpha_slot[first_block : first_block + per_batch],
            alpha_pair[first_block : first_block + per_batch],
            alpha_parity[first_block : first_block + per_batch],
        )

        def one_entry(item):
            return block_sigma(
                received, item[0], item[1], item[2], integrals, pair_table, beta_blocks
            )

        results = lax.map(one_entry, entries)
        partial_rows = results.reshape(per_batch * SB, beta_blocks * BBLK)
        outputs.append(lax.psum_scatter(partial_rows, "beta", scatter_dimension=1, tiled=True))
    return jnp.concatenate(outputs, axis=0)


def solution(mesh):
    in_specs = (
        P("alpha", "beta"),
        P(),
        P("alpha", None),
        P("alpha", None),
        P("alpha", None),
        P("alpha", None),
        P("beta", None),
        P("beta", None),
        P("beta", None),
    )
    out_specs = P("alpha", "beta")
    return jax.shard_map(
        on_device, mesh=mesh, in_specs=in_specs, out_specs=out_specs, check_vma=False
    )
```

profile of v0, /device:TPU:1, one launch (start us, length us, event | category | flops | bytes accessed | tf_op | source)
XLA Modules:
  0.0 148.5 jit_solution(13568207810081582431)
XLA Ops:
  10.2 12.0 %all-to-all-start = ((bf16[64,4,1024]{2,1,0:T(4,128)(2,1)}), bf16[64,4,1024]{2,1,0:T(4,128)(2,1)S(1)}, u32[]{:S(2)}, u32[]{:S(2)}) async-start(bf16[64,4,1024]{2,1,0:T(4,128)(2,1)} %all_to_all.16), calls=%async_computation | async-start | bytes 1048576 | tf_op jit(solution)/shard_map/all_to_all | solution.py:72
  24.5 1.9 %fusion.32 = f32[16,32,484]{2,1,0:T(8,128)S(1)} fusion(s32[16,132]{1,0:T(8,128)S(1)} %copy-done.4, f32[16,132]{1,0:T(8,128)S(1)} %subtract_convert_fusion, s32[16,132]{1,0:T(8,128)S(1)} %copy-done.5), kind=kOutput, calls=%fused_computation.45 | convolution fusion | flops 393685248 | bytes 1016576 | tf_op jit(solution)/shard_map/veu,vep->vup/dot_general | solution.py:66
  26.4 8.0 %all-to-all-done = bf16[64,4,1024]{2,1,0:T(4,128)(2,1)S(1)} async-done(((bf16[64,4,1024]{2,1,0:T(4,128)(2,1)}), bf16[64,4,1024]{2,1,0:T(4,128)(2,1)S(1)}, u32[]{:S(2)}, u32[]{:S(2)}) %all-to-all-start) | async-done | bytes 524320 | tf_op jit(solution)/shard_map/all_to_all | solution.py:72
  34.4 5.5 %all-to-all-start.1 = ((bf16[64,4,1024]{2,1,0:T(4,128)(2,1)}), bf16[64,4,1024]{2,1,0:T(4,128)(2,1)}, u32[]{:S(2)}, u32[]{:S(2)}) async-start(bf16[64,4,1024]{2,1,0:T(4,128)(2,1)} %all_to_all.19), calls=%async_computation.2 | async-start | bytes 1048576 | tf_op jit(solution)/shard_map/all_to_all | solution.py:72
  40.9 41.2 %while.20 = (s32[]{:T(128)}, f32[8,4,512]{2,1,0:T(4,128)S(1)}, s32[8,132]{1,0:T(8,128)S(1)}, bf16[484,484]{1,0:T(8,128)(2,1)}, s32[8,132]{1,0:T(8,128)S(1)}, /*i...) while((s32[]{:T(128)}, f32[8,4,512]{2,1,0:T(4,128)S(1)}, ...), condition=%wide.region_1.2_spmd, body=%wide.region_0.1_spmd.sunk | while | flops 452603584 | bytes 6266713 | solution.py:85
  42.3 1.8 %fusion.73 = f32[484,1024]{0,1:T(8,128)S(1)} fusion(bf16[132,484]{1,0:T(8,128)(2,1)S(1)} %convolution_convert_fusion.6, bf16[256,1024]{1,0:T(8,128)(2,1)} %get-tuple-element.294, f32[132]{0:T(256)S(1)} %bitcast.80, s32[132]{0:T(256)S(1)} %bitcast.82), kind=kOutput, calls=%fused_computation.3.clone.1 | convolution fusion | flops 200251392 | bytes 2635584 | tf_op jit(solution)/shard_map/while/body/eval_jaxpr/dot_general | solution.py:29
  47.4 1.8 %fusion.73 = f32[484,1024]{0,1:T(8,128)S(1)} fusion(bf16[132,484]{1,0:T(8,128)(2,1)S(1)} %convolution_convert_fusion.6, bf16[256,1024]{1,0:T(8,128)(2,1)} %get-tuple-element.294, f32[132]{0:T(256)S(1)} %bitcast.80, s32[132]{0:T(256)S(1)} %bitcast.82), kind=kOutput, calls=%fused_computation.3.clone.1 | convolution fusion | flops 200251392 | bytes 2635584 | tf_op jit(solution)/shard_map/while/body/eval_jaxpr/dot_general | solution.py:29
  54.4 1.8 %convolution_bitcast_fusion.4 = f32[4,32,16]{1,2,0:T(8,128)S(1)} fusion(f32[484,4,16,16]{0,3,2,1:T(8,128)S(1)} %bitcast.78, f32[16,32,484]{2,1,0:T(8,128)S(1)} %get-tuple-element.295), kind=kOutput, calls=%fused_computation.5.clone.1 | convolution fusion | flops 190316544 | bytes 2981888 | tf_op jit(solution)/shard_map/while/body/eval_jaxpr/vup,psvb->sub/dot_general | solution.py:32
  57.7 1.8 %fusion.73 = f32[484,1024]{0,1:T(8,128)S(1)} fusion(bf16[132,484]{1,0:T(8,128)(2,1)S(1)} %convolution_convert_fusion.6, bf16[256,1024]{1,0:T(8,128)(2,1)} %get-tuple-element.294, f32[132]{0:T(256)S(1)} %bitcast.80, s32[132]{0:T(256)S(1)} %bitcast.82), kind=kOutput, calls=%fused_computation.3.clone.1 | convolution fusion | flops 200251392 | bytes 2635584 | tf_op jit(solution)/shard_map/while/body/eval_jaxpr/dot_general | solution.py:29
  62.9 1.8 %fusion.73 = f32[484,1024]{0,1:T(8,128)S(1)} fusion(bf16[132,484]{1,0:T(8,128)(2,1)S(1)} %convolution_convert_fusion.6, bf16[256,1024]{1,0:T(8,128)(2,1)} %get-tuple-element.294, f32[132]{0:T(256)S(1)} %bitcast.80, s32[132]{0:T(256)S(1)} %bitcast.82), kind=kOutput, calls=%fused_computation.3.clone.1 | convolution fusion | flops 200251392 | bytes 2635584 | tf_op jit(solution)/shard_map/while/body/eval_jaxpr/dot_general | solution.py:29
  68.0 1.8 %fusion.73 = f32[484,1024]{0,1:T(8,128)S(1)} fusion(bf16[132,484]{1,0:T(8,128)(2,1)S(1)} %convolution_convert_fusion.6, bf16[256,1024]{1,0:T(8,128)(2,1)} %get-tuple-element.294, f32[132]{0:T(256)S(1)} %bitcast.80, s32[132]{0:T(256)S(1)} %bitcast.82), kind=kOutput, calls=%fused_computation.3.clone.1 | convolution fusion | flops 200251392 | bytes 2635584 | tf_op jit(solution)/shard_map/while/body/eval_jaxpr/dot_general | solution.py:29
  73.2 1.8 %fusion.73 = f32[484,1024]{0,1:T(8,128)S(1)} fusion(bf16[132,484]{1,0:T(8,128)(2,1)S(1)} %convolution_convert_fusion.6, bf16[256,1024]{1,0:T(8,128)(2,1)} %get-tuple-element.294, f32[132]{0:T(256)S(1)} %bitcast.80, s32[132]{0:T(256)S(1)} %bitcast.82), kind=kOutput, calls=%fused_computation.3.clone.1 | convolution fusion | flops 200251392 | bytes 2635584 | tf_op jit(solution)/shard_map/while/body/eval_jaxpr/dot_general | solution.py:29
  78.3 1.8 %fusion.73 = f32[484,1024]{0,1:T(8,128)S(1)} fusion(bf16[132,484]{1,0:T(8,128)(2,1)S(1)} %convolution_convert_fusion.6, bf16[256,1024]{1,0:T(8,128)(2,1)} %get-tuple-element.294, f32[132]{0:T(256)S(1)} %bitcast.80, s32[132]{0:T(256)S(1)} %bitcast.82), kind=kOutput, calls=%fused_computation.3.clone.1 | convolution fusion | flops 200251392 | bytes 2635584 | tf_op jit(solution)/shard_map/while/body/eval_jaxpr/dot_general | solution.py:29
  82.8 2.0 %all_to_all.21 = bf16[256,1024]{1,0:T(8,128)(2,1)} reshape(bf16[64,4,1024]{2,1,0:T(4,128)(2,1)} %all-to-all-done.1) | data formatting | bytes 1048576 | tf_op jit(solution)/shard_map/all_to_all | solution.py:72
  84.8 41.2 %while.21 = (s32[]{:T(128)}, f32[8,4,512]{2,1,0:T(4,128)S(1)}, s32[8,132]{1,0:T(8,128)S(1)}, bf16[484,484]{1,0:T(8,128)(2,1)}, s32[8,132]{1,0:T(8,128)S(1)}, /*i...) while((s32[]{:T(128)}, f32[8,4,512]{2,1,0:T(4,128)S(1)}, ...), condition=%wide.region_4.5_spmd, body=%wide.region_3.4_spmd.sunk | while | flops 452603584 | bytes 6266713 | solution.py:85
  86.2 1.8 %fusion.81 = f32[484,1024]{0,1:T(8,128)S(1)} fusion(bf16[132,484]{1,0:T(8,128)(2,1)S(1)} %convolution_convert_fusion.7, bf16[256,1024]{1,0:T(8,128)(2,1)} %get-tuple-element.267, f32[132]{0:T(256)S(1)} %bitcast.81, s32[132]{0:T(256)S(1)} %bitcast.83), kind=kOutput, calls=%fused_computation.24.clone.1 | convolution fusion | flops 200251392 | bytes 2635584 | tf_op jit(solution)/shard_map/while/body/eval_jaxpr/dot_general | solution.py:29
  93.1 1.8 %convolution_bitcast_fusion.5 = f32[4,32,16]{1,2,0:T(8,128)S(1)} fusion(f32[484,4,16,16]{0,3,2,1:T(8,128)S(1)} %bitcast.79, f32[16,32,484]{2,1,0:T(8,128)S(1)} %get-tuple-element.268), kind=kOutput, calls=%fused_computation.26.clone.1 | convolution fusion | flops 190316544 | bytes 2981888 | tf_op jit(solution)/shard_map/while/body/eval_jaxpr/vup,psvb->sub/dot_general | solution.py:32
  96.5 1.8 %fusion.81 = f32[484,1024]{0,1:T(8,128)S(1)} fusion(bf16[132,484]{1,0:T(8,128)(2,1)S(1)} %convolution_convert_fusion.7, bf16[256,1024]{1,0:T(8,128)(2,1)} %get-tuple-element.267, f32[132]{0:T(256)S(1)} %bitcast.81, s32[132]{0:T(256)S(1)} %bitcast.83), kind=kOutput, calls=%fused_computation.24.clone.1 | convolution fusion | flops 200251392 | bytes 2635584 | tf_op jit(solution)/shard_map/while/body/eval_jaxpr/dot_general | solution.py:29
  101.7 1.8 %fusion.81 = f32[484,1024]{0,1:T(8,128)S(1)} fusion(bf16[132,484]{1,0:T(8,128)(2,1)S(1)} %convolution_convert_fusion.7, bf16[256,1024]{1,0:T(8,128)(2,1)} %get-tuple-element.267, f32[132]{0:T(256)S(1)} %bitcast.81, s32[132]{0:T(256)S(1)} %bitcast.83), kind=kOutput, calls=%fused_computation.24.clone.1 | convolution fusion | flops 200251392 | bytes 2635584 | tf_op jit(solution)/shard_map/while/body/eval_jaxpr/dot_general | solution.py:29
  106.8 1.8 %fusion.81 = f32[484,1024]{0,1:T(8,128)S(1)} fusion(bf16[132,484]{1,0:T(8,128)(2,1)S(1)} %convolution_convert_fusion.7, bf16[256,1024]{1,0:T(8,128)(2,1)} %get-tuple-element.267, f32[132]{0:T(256)S(1)} %bitcast.81, s32[132]{0:T(256)S(1)} %bitcast.83), kind=kOutput, calls=%fused_computation.24.clone.1 | convolution fusion | flops 200251392 | bytes 2635584 | tf_op jit(solution)/shard_map/while/body/eval_jaxpr/dot_general | solution.py:29
  112.0 1.8 %fusion.81 = f32[484,1024]{0,1:T(8,128)S(1)} fusion(bf16[132,484]{1,0:T(8,128)(2,1)S(1)} %convolution_convert_fusion.7, bf16[256,1024]{1,0:T(8,128)(2,1)} %get-tuple-element.267, f32[132]{0:T(256)S(1)} %bitcast.81, s32[132]{0:T(256)S(1)} %bitcast.83), kind=kOutput, calls=%fused_computation.24.clone.1 | convolution fusion | flops 200251392 | bytes 2635584 | tf_op jit(solution)/shard_map/while/body/eval_jaxpr/dot_general | solution.py:29
  117.1 1.8 %fusion.81 = f32[484,1024]{0,1:T(8,128)S(1)} fusion(bf16[132,484]{1,0:T(8,128)(2,1)S(1)} %convolution_convert_fusion.7, bf16[256,1024]{1,0:T(8,128)(2,1)} %get-tuple-element.267, f32[132]{0:T(256)S(1)} %bitcast.81, s32[132]{0:T(256)S(1)} %bitcast.83), kind=kOutput, calls=%fused_computation.24.clone.1 | convolution fusion | flops 200251392 | bytes 2635584 | tf_op jit(solution)/shard_map/while/body/eval_jaxpr/dot_general | solution.py:29
  122.3 1.8 %fusion.81 = f32[484,1024]{0,1:T(8,128)S(1)} fusion(bf16[132,484]{1,0:T(8,128)(2,1)S(1)} %convolution_convert_fusion.7, bf16[256,1024]{1,0:T(8,128)(2,1)} %get-tuple-element.267, f32[132]{0:T(256)S(1)} %bitcast.81, s32[132]{0:T(256)S(1)} %bitcast.83), kind=kOutput, calls=%fused_computation.24.clone.1 | convolution fusion | flops 200251392 | bytes 2635584 | tf_op jit(solution)/shard_map/while/body/eval_jaxpr/dot_general | solution.py:29
  126.7 13.5 %reduce-scatter.5.cloned.1.call-done = f32[32,256]{1,0:T(8,128)} async-done(((f32[32,512]{1,0:T(8,128)}), f32[32,256]{1,0:T(8,128)}) %reduce-scatter.5.cloned.1.call-update) | async-done | bytes 32784 | tf_op jit(solution)/shard_map/reduce_scatter | solution.py:87
  (148 shorter events, 62.9 us)
Async XLA Ops:
  9.2 13.0 %copy-start = (s32[16,132]{1,0:T(8,128)S(1)}, s32[16,132]{1,0:T(8,128)}, u32[]{:S(2)}) copy-start(s32[16,132]{1,0:T(8,128)} %param.21) | copy-start | bytes 25348
  9.2 13.0 %copy-start.1 = (s32[16,132]{1,0:T(8,128)S(1)}, s32[16,132]{1,0:T(8,128)}, u32[]{:S(2)}) copy-start(s32[16,132]{1,0:T(8,128)} %param.17) | copy-start | bytes 25348
  10.2 24.1 %all-to-all-start = ((bf16[64,4,1024]{2,1,0:T(4,128)(2,1)}), bf16[64,4,1024]{2,1,0:T(4,128)(2,1)S(1)}, u32[]{:S(2)}, u32[]{:S(2)}) async-start(bf16[64,4,1024]{2,1,0:T(4,128)(2,1)} %all_to_all.16), calls=%async_computation | async-start | bytes 1048576 | tf_op jit(solution)/shard_map/all_to_all | solution.py:72
  22.3 2.2 %copy-start.2 = (s32[16,132]{1,0:T(8,128)S(1)}, s32[16,132]{1,0:T(8,128)}, u32[]{:S(2)}) copy-start(s32[16,132]{1,0:T(8,128)} %param.18) | copy-start | bytes 25348
  22.3 2.2 %copy-start.3 = (s32[16,132]{1,0:T(8,128)S(1)}, s32[16,132]{1,0:T(8,128)}, u32[]{:S(2)}) copy-start(s32[16,132]{1,0:T(8,128)} %param.16) | copy-start | bytes 25348
  22.3 2.2 %copy-start.4 = (s32[16,132]{1,0:T(8,128)S(1)}, s32[16,132]{1,0:T(8,128)}, u32[]{:S(2)}) copy-start(s32[16,132]{1,0:T(8,128)} %param.19) | copy-start | bytes 25348
  22.3 2.2 %copy-start.5 = (s32[16,132]{1,0:T(8,128)S(1)}, s32[16,132]{1,0:T(8,128)}, u32[]{:S(2)}) copy-start(s32[16,132]{1,0:T(8,128)} %param.20) | copy-start | bytes 25348
  34.4 48.5 %all-to-all-start.1 = ((bf16[64,4,1024]{2,1,0:T(4,128)(2,1)}), bf16[64,4,1024]{2,1,0:T(4,128)(2,1)}, u32[]{:S(2)}, u32[]{:S(2)}) async-start(bf16[64,4,1024]{2,1,0:T(4,128)(2,1)} %all_to_all.19), calls=%async_computation.2 | async-start | bytes 1048576 | tf_op jit(solution)/shard_map/all_to_all | solution.py:72
  39.9 86.9 %reduce-scatter.3.cloned.1.call-start = ((), (), s32[]{:S(2)}) async-start(), calls=%async_computation.4 | async-start | bytes 98304 | tf_op jit(solution)/shard_map/reduce_scatter | solution.py:87
  82.8 57.5 %reduce-scatter.5.cloned.1.call-start = ((), (), s32[]{:S(2)}) async-start(), calls=%async_computation.5 | async-start | bytes 98304 | tf_op jit(solution)/shard_map/reduce_scatter | solution.py:87
Sparse Core Ops, SparseCore 0:
  82.9 13.4 reduce-scatter.2
  126.8 13.3 reduce-scatter.4
where the time goes:
time: 150 us; the launch traced here: 148 us
  matrix products  80.1 us (53%)
  waiting for transfers between devices  21.5 us (14%)
  starting transfers between devices  17.5 us (12%)
  between operations  13.6 us (9%)
  local copies, waits for them, and re-layouts  12.6 us (8%)
  other arithmetic  2.34 us (2%)
    dot_general x16, matrix products, block_sigma(): contracted = jnp.dot(selected, signed, preferred_element_type=jnp.float32)  28.4 us
    dot_general x16, matrix products, block_sigma(): jnp.einsum('vup,psvb->sub', pair_table, arranged, precision=lax.Precision...  28.3 us
    dot_general x16, matrix products, block_sigma(): jnp.dot(integrals, pair_hot, preferred_element_type=jnp.float32)  21.6 us
    all_to_all x2, starting transfers between devices, on_device(): lax.all_to_all(outgoing, 'alpha', split_axis=0, concat_axis=0, tiled=True)  17.5 us
    reduce_scatter x2, waiting for transfers between devices, on_device(): lax.psum_scatter(partial_rows, 'beta', scatter_dimension=1, tiled=True)  13.5 us
    all_to_all x2, waiting for transfers between devices, on_device(): lax.all_to_all(outgoing, 'alpha', split_axis=0, concat_axis=0, tiled=True)  7.96 us
    all_to_all x4, local copies, waits for them, and re-layouts, on_device(): lax.all_to_all(outgoing, 'alpha', split_axis=0, concat_axis=0, tiled=True)  4.9 us
  transfers between devices with their start and end apart: 4, of which 2 were waited for; matrix products, arithmetic and copies ran while one was open for 58% of the time, Pallas kernels for 0%

commit v1 on v0

v1 whole, which is shorter than its diff:
```python
import functools

import jax
import jax.numpy as jnp
from jax import lax
from jax.experimental import pallas as pl
from jax.experimental.pallas import tpu as pltpu
from jax.sharding import PartitionSpec as P

MESH = pl.DeviceIdType.MESH
PAIRS = 484
PPAD = 512
EXC = 132
EPAD = 136
SB = 4
BATCHES = 2
CAP = 4
NV = 16
NU = 32
NG = 16
GB = 8
NS = 64
WCH = 8
SLOTS = NS * CAP
F32 = jnp.float32
BF16 = jnp.bfloat16


def kernel(
    coeffs_ref,
    integrals_ref,
    send_ref,
    aslot_ref,
    apair_ref,
    apar_ref,
    bpair_ref,
    btarget_ref,
    bpar_ref,
    out_ref,
    cscr,
    src,
    dst,
    tab,
    codes,
    tscr,
    ipad,
    wscr,
    alhs,
    xscr,
    part,
    rpart,
    ssem,
    rsem,
    lsem,
    psem,
    qsem,
):
    a = lax.axis_index("alpha")
    b = lax.axis_index("beta")
    partner = (a, 1 - b)
    barrier = pltpu.get_barrier_semaphore()

    def signal_peer(k, carry):
        pl.semaphore_signal(barrier, inc=1, device_id=(lax.rem(a + k, NS), b), device_id_type=MESH)
        return carry

    lax.fori_loop(1, NS, signal_peer, 0)
    pl.semaphore_signal(barrier, inc=1, device_id=partner, device_id_type=MESH)

    for h in range(2):
        cscr[h] = coeffs_ref[:, h * 128 : (h + 1) * 128].astype(F32)
    lane_group = lax.broadcasted_iota(jnp.int32, (16, 128), 1) // 16
    pieces = [
        [cscr.at[h][pl.ds(s, 16, stride=SB), :] for h in range(2)] for s in range(SB)
    ]
    columns = []
    for w in range(WCH):
        value = jnp.zeros((16, 128), F32)
        for par in range(2):
            v = 2 * w + par
            for s in range(SB):
                shift = ((par * 4 + s) - (v % 8)) % 8 * 16
                piece = pieces[s][v // 8]
                moved = pltpu.roll(piece, shift, 1) if shift else piece
                value = jnp.where(lane_group == par * 4 + s, moved, value)
        columns.append(value.astype(BF16))
    blocks = jnp.concatenate(columns, axis=1)
    for batch in range(BATCHES):
        wanted = send_ref[:, pl.ds(batch * SLOTS, SLOTS)]
        hot = (lax.broadcasted_iota(jnp.int32, (16, SLOTS), 0) == wanted).astype(F32)
        picked = jnp.dot(hot.T.astype(BF16), blocks, preferred_element_type=F32).astype(BF16)
        for w in range(WCH):
            src[batch, w] = picked[:, w * 128 : (w + 1) * 128].reshape(NS, CAP, 128)

    pl.semaphore_wait(barrier, NS)

    def block_copy(batch, to):
        return pltpu.make_async_remote_copy(
            src_ref=src.at[batch, :, to],
            dst_ref=dst.at[batch, :, a],
            send_sem=ssem.at[batch],
            recv_sem=rsem.at[batch],
            device_id=(to, b),
            device_id_type=MESH,
        )

    for batch in range(BATCHES):

        def send(k, carry):
            block_copy(batch, lax.rem(a + k, NS)).start()
            return carry

        lax.fori_loop(1, NS, send, 0)
    own = [
        pltpu.make_async_copy(src.at[batch, :, a], dst.at[batch, :, a], lsem.at[batch])
        for batch in range(BATCHES)
    ]
    for copy in own:
        copy.start()

    tab[...] = jnp.full(tab.shape, -1.0, F32)
    tab[0, :, 0:EXC] = bpair_ref[...].astype(F32)
    tab[1, :, 0:EXC] = ((1 - 2 * bpar_ref[...]) * (btarget_ref[...] + 1)).astype(F32)
    tab[2, :, 0:EXC] = apair_ref[...].astype(F32)
    tab[3, :, 0:EXC] = ((1 - 2 * apar_ref[...]) * (aslot_ref[...] + 1)).astype(F32)
    pair_lane = lax.broadcasted_iota(jnp.int32, (EPAD, PPAD), 1).astype(F32)
    for side in range(2):
        pair_cols = tab[2 * side].T[0:EPAD]
        code_cols = tab[2 * side + 1].T[0:EPAD]
        for row in range(NV):
            hit = pair_cols[:, row : row + 1] == pair_lane
            codes[side, row] = jnp.sum(
                jnp.where(hit, code_cols[:, row : row + 1], 0.0), axis=0, keepdims=True
            )

    def signed_hot(code, count):
        place = (lax.broadcasted_iota(jnp.int32, (count, PPAD), 0) + 1).astype(F32)
        return (jnp.where(code == place, 1.0, 0.0) - jnp.where(code == -place, 1.0, 0.0)).astype(
            BF16
        )

    def beta_row(v, carry):
        tscr[pl.ds(pl.multiple_of(v * NU, NU), NU), :] = signed_hot(codes[0, v], NU)
        return carry

    lax.fori_loop(0, NV, beta_row, 0)
    ipad[...] = jnp.zeros(ipad.shape, BF16)
    ipad[0:PAIRS, 0:PAIRS] = integrals_ref[...]
    table = jnp.dot(tscr[...], ipad[...], preferred_element_type=F32)
    high = table.astype(BF16)
    wscr[:, 0:PPAD] = high
    wscr[:, PPAD:] = (table - high.astype(F32)).astype(BF16)

    def alpha_row(g, carry):
        hot = signed_hot(codes[1, g], SLOTS)
        product = lax.dot_general(
            wscr[...],
            jnp.concatenate([hot, hot], axis=1),
            (((1,), (1,)), ((), ())),
            preferred_element_type=F32,
        )
        top = product.astype(BF16)
        rest = (product - top.astype(F32)).astype(BF16)
        batch, local = g // GB, lax.rem(g, GB)
        for v in range(NV):
            rows = slice(v * NU, (v + 1) * NU)
            lanes = slice((v // 2) * SLOTS, (v // 2 + 1) * SLOTS)
            alhs[batch, v % 2, local, 0, :, lanes] = top[rows]
            alhs[batch, v % 2, local, 1, :, lanes] = rest[rows]
        return carry

    lax.fori_loop(0, NG, alpha_row, 0)

    small_group = lax.broadcasted_iota(jnp.int32, (GB, 128), 1) // 16
    for batch in range(BATCHES):
        own[batch].wait()
        arrived = pltpu.make_async_remote_copy(
            src_ref=src.at[batch, :, pl.ds(0, NS - 1)],
            dst_ref=dst.at[batch, :, pl.ds(0, NS - 1)],
            send_sem=ssem.at[batch],
            recv_sem=rsem.at[batch],
            device_id=partner,
            device_id_type=MESH,
        )
        arrived.wait_recv()
        right = dst[batch].reshape(WCH * SLOTS, 128)
        left = alhs[batch].reshape(2 * GB * 2 * NU, WCH * SLOTS)
        result = jnp.dot(left, right, preferred_element_type=F32).reshape(2, GB, 2, NU, 128)
        result = result[:, :, 0] + result[:, :, 1]
        even = result[0].reshape(GB * NU, 128)
        odd = result[1].reshape(GB * NU, 128)
        xscr[...] = even + pltpu.roll(odd, 64, 1)
        for j in range(4):
            by_u = [xscr[pl.ds(8 * j + i, GB, stride=NU), :] for i in range(8)]
            total = [jnp.zeros((GB, 128), F32) for _ in range(SB)]
            for d in range(8):
                mixed = by_u[d % 8]
                for s in range(1, SB):
                    mixed = jnp.where(small_group == s, by_u[(s + d) % 8], mixed)
                moved = pltpu.roll(mixed, 16 * d, 1) if d else mixed
                for s in range(SB):
                    total[s] = jnp.where(small_group == (s + d) % 8, moved, total[s])
            for s in range(SB):
                part.at[j // 2, j % 2][pl.ds(batch * GB * SB + s, GB, stride=SB), :] = total[s]

    swap = pltpu.make_async_remote_copy(
        src_ref=part.at[1 - b],
        dst_ref=rpart,
        send_sem=psem,
        recv_sem=qsem,
        device_id=partner,
        device_id_type=MESH,
    )
    swap.start()
    for batch in range(BATCHES):
        pltpu.make_async_remote_copy(
            src_ref=src.at[batch, :, pl.ds(0, NS - 1)],
            dst_ref=dst.at[batch, :, pl.ds(0, NS - 1)],
            send_sem=ssem.at[batch],
            recv_sem=rsem.at[batch],
            device_id=partner,
            device_id_type=MESH,
        ).wait_send()
    swap.wait()
    for h in range(2):
        out_ref[:, h * 128 : (h + 1) * 128] = part[b, h] + rpart[h]


def on_device(*operands):
    vmem = pl.BlockSpec(memory_space=pltpu.VMEM)
    return pl.pallas_call(
        kernel,
        out_shape=jax.ShapeDtypeStruct((64, 256), F32),
        in_specs=[vmem] * 9,
        out_specs=vmem,
        scratch_shapes=[
            pltpu.VMEM((2, 64, 128), F32),
            pltpu.VMEM((BATCHES, WCH, NS, CAP, 128), BF16),
            pltpu.VMEM((BATCHES, WCH, NS, CAP, 128), BF16),
            pltpu.VMEM((4, 16, 256), F32),
            pltpu.VMEM((2, NV, 1, PPAD), F32),
            pltpu.VMEM((NV * NU, PPAD), BF16),
            pltpu.VMEM((PPAD, PPAD), BF16),
            pltpu.VMEM((NV * NU, 2 * PPAD), BF16),
            pltpu.VMEM((BATCHES, 2, GB, 2, NU, WCH * SLOTS), BF16),
            pltpu.VMEM((GB * NU, 128), F32),
            pltpu.VMEM((2, 2, 64, 128), F32),
            pltpu.VMEM((2, 64, 128), F32),
            pltpu.SemaphoreType.DMA((BATCHES,)),
            pltpu.SemaphoreType.DMA((BATCHES,)),
            pltpu.SemaphoreType.DMA((BATCHES,)),
            pltpu.SemaphoreType.DMA,
            pltpu.SemaphoreType.DMA,
        ],
        compiler_params=pltpu.CompilerParams(
            collective_id=0, has_side_effects=True, vmem_limit_bytes=56 << 20
        ),
    )(*operands)


def solution(mesh):
    in_specs = (
        P("alpha", "beta"),
        P(),
        P("alpha", None),
        P("alpha", None),
        P("alpha", None),
        P("alpha", None),
        P("beta", None),
        P("beta", None),
        P("beta", None),
    )
    return jax.shard_map(
        on_device, mesh=mesh, in_specs=in_specs, out_specs=P("alpha", "beta"), check_vma=False
    )
```

time: 150 us -> 33.4 us (0.22)
  matrix products: 80.1 us -> 0 us
  Pallas kernels: 0 us -> 31.7 us
  waiting for transfers between devices: 21.5 us -> 0 us
  starting transfers between devices: 17.5 us -> 0 us
  between operations: 13.6 us -> 0.01 us
  local copies, waits for them, and re-layouts: 12.6 us -> 1.47 us
  other arithmetic: 2.34 us -> 0 us
    dot_general x49 -> x0, matrix products: 80.1 us -> none  [the longest x16 28.4 us: block_sigma(): contracted = jnp.dot(selected, signed, preferred_element_type=jnp.float32)]
    pallas_call x0 -> x1, Pallas kernels: none -> 31.7 us  [on_device(): pl.pallas_call(kernel, out_shape=jax.ShapeDtypeStruct((64, 256), F32), in...]
    all_to_all x2 -> x0, starting transfers between devices: 17.5 us -> none  [on_device(): lax.all_to_all(outgoing, 'alpha', split_axis=0, concat_axis=0, tiled=True)]
    reduce_scatter x2 -> x0, waiting for transfers between devices: 13.5 us -> none  [on_device(): lax.psum_scatter(partial_rows, 'beta', scatter_dimension=1, tiled=True)]
    all_to_all x2 -> x0, waiting for transfers between devices: 7.96 us -> none  [on_device(): lax.all_to_all(outgoing, 'alpha', split_axis=0, concat_axis=0, tiled=True)]
    all_to_all x4 -> x0, local copies, waits for them, and re-layouts: 4.9 us -> none  [on_device(): lax.all_to_all(outgoing, 'alpha', split_axis=0, concat_axis=0, tiled=True)]
    gather x2 -> x0, local copies, waits for them, and re-layouts: 2.34 us -> none  [on_device(): outgoing = padded[send_lists[batch_index]]]
    reshape x3 -> x0, local copies, waits for them, and re-layouts: 2.08 us -> none  [the longest x2 1.29 us: on_device(): partial_rows = results.reshape(per_batch * SB, beta_blocks * BBLK)]
  transfers between devices with their start and end apart: 4 -> 0, of which waited for: 2 -> 0; matrix products, arithmetic and copies ran while one was open for 58% -> 0% of each run, Pallas kernels for 0% -> 0%
where the time goes in v1:
time: 33.4 us; the launch traced here: 33.2 us
  Pallas kernels  31.7 us (95%)
  local copies, waits for them, and re-layouts  1.47 us (4%)
    pallas_call x1, Pallas kernels, on_device(): pl.pallas_call(kernel, out_shape=jax.ShapeDtypeStruct((64, 256), F32), in...  31.7 us
    unnamed x1, local copies, waits for them, and re-layouts  1.47 us

profile of v1, /device:TPU:1, one launch (start us, length us, event | category | flops | bytes accessed | tf_op | source)
XLA Modules:
  0.0 33.2 jit_solution(4768841317394003986)
XLA Ops:
  0.0 31.7 %shard_map.91 = f32[64,256]{1,0:T(8,128)} custom-call(bf16[64,256]{1,0:T(8,128)(2,1)} %coeffs_ref.1, bf16[484,484]{1,0:T(8,128)(2,1)} %integrals_ref.1, s32[1,512]{1,0:T(1,128)} %send_ref.1, s32[16,132]{1,0:T(8,128)} %aslot_ref.1, s32[16,132]{1,0:T(8,128)} %apair_ref.1, s32[16,132]{1,0:T(8,128)} %apar_ref.1, s32[16,132]{1,0:T(8,128)} %bpair_ref.1, ...), custom_call_target="tpu_custom_call" | custom-call | tf_op jit(solution)/shard_map/pallas_call | solution.py:231
  31.8 1.5 %copy.11 = f32[64,256]{1,0:T(8,128)} copy(f32[64,256]{1,0:T(8,128)} %shard_map.91) | data formatting | bytes 131072

commit v2 on v1

v2 whole, which is shorter than its diff:
```python
import functools

import jax
import jax.numpy as jnp
from jax import lax
from jax.experimental import pallas as pl
from jax.experimental.pallas import tpu as pltpu
from jax.sharding import PartitionSpec as P

MESH = pl.DeviceIdType.MESH
PAIRS = 484
PPAD = 512
EXC = 132
EPAD = 136
SB = 4
BATCHES = 2
CAP = 4
NV = 16
NU = 32
NG = 16
GB = 8
NS = 64
X_LINE, Y_LINE, Z_LINE = (1, 2, 3), (4, 8, 12), (16, 32, 48)
LINES = X_LINE + Y_LINE + Z_LINE


def dims_of(k):
    return (k % 4 > 0) + (k // 4 % 4 > 0) + (k // 16 > 0)


PLANES = tuple(k for k in range(1, 64) if dims_of(k) == 2)
REST = tuple(k for k in range(1, 64) if dims_of(k) == 3)
CHUNKS = ((0, 0, 8), (1, 0, 4), (1, 4, 4))
WCH = 8
SLOTS = NS * CAP
GSTEP = 4
F32 = jnp.float32
BF16 = jnp.bfloat16


def kernel(
    coeffs_ref,
    integrals_ref,
    send_ref,
    aslot_ref,
    apair_ref,
    apar_ref,
    bpair_ref,
    btarget_ref,
    bpar_ref,
    own_ref,
    far_ref,
    coeffs,
    integrals,
    sends,
    small,
    cscr,
    src,
    dst,
    tab,
    codes,
    tscr,
    ipad,
    wscr,
    alhs,
    hots,
    fsum,
    xscr,
    part,
    near_sem,
    wide_sem,
    insem,
    ssem,
    rsem,
    lsem,
    ksem,
    psem,
    qsem,
):
    a = lax.axis_index("alpha")
    b = lax.axis_index("beta")
    partner = (a, 1 - b)

    here = (lax.div(a, 16), lax.rem(lax.div(a, 4), 4), lax.rem(a, 4))
    steps = [[lax.rem(place + i, 4) * scale for i in range(4)] for place, scale in zip(here, (16, 4, 1))]

    def peer(k):
        return steps[0][k // 16] + (steps[1][k // 4 % 4] + steps[2][k % 4])

    barrier = pltpu.get_barrier_semaphore()
    loads = [
        pltpu.make_async_copy(ref, to, insem.at[i])
        for i, (ref, to) in enumerate(
            [(coeffs_ref, coeffs), (send_ref, sends)]
            + [
                (ref, small.at[i])
                for i, ref in enumerate(
                    [bpair_ref, btarget_ref, bpar_ref, apair_ref, aslot_ref, apar_ref]
                )
            ]
            + [(integrals_ref, integrals)]
        )
    ]
    for load in loads:
        load.start()

    def tell(semaphore, k):
        pl.semaphore_signal(semaphore, inc=1, device_id=(peer(k), b), device_id_type=MESH)

    for k in LINES:
        tell(barrier, k)
    pl.semaphore_signal(barrier, inc=1, device_id=partner, device_id_type=MESH)

    loads[0].wait()
    loads[1].wait()
    for h in range(2):
        cscr[h] = coeffs[:, h * 128 : (h + 1) * 128].astype(F32)
    lane_group = lax.broadcasted_iota(jnp.int32, (16, 128), 1) // 16
    pieces = [
        [cscr.at[h][pl.ds(s, 16, stride=SB), :] for h in range(2)] for s in range(SB)
    ]
    columns = []
    for w in range(WCH):
        value = jnp.zeros((16, 128), F32)
        for par in range(2):
            v = 2 * w + par
            for s in range(SB):
                shift = ((par * 4 + s) - (v % 8)) % 8 * 16
                piece = pieces[s][v // 8]
                moved = pltpu.roll(piece, shift, 1) if shift else piece
                value = jnp.where(lane_group == par * 4 + s, moved, value)
        columns.append(value.astype(BF16))
    blocks = jnp.concatenate(columns, axis=1)
    for batch in range(BATCHES):
        wanted = sends[:, pl.ds(batch * SLOTS, SLOTS)]
        hot = (lax.broadcasted_iota(jnp.int32, (16, SLOTS), 0) == wanted).astype(F32)
        picked = jnp.dot(hot.T.astype(BF16), blocks, preferred_element_type=F32).astype(BF16)
        for w in range(WCH):
            src[batch, w] = picked[:, w * 128 : (w + 1) * 128].reshape(NS, CAP, 128)

    pl.semaphore_wait(barrier, len(LINES) + 1)

    def block_copy(q, to):
        batch, first, count = CHUNKS[q]
        cols = pl.ds(first, count)
        return pltpu.make_async_remote_copy(
            src_ref=src.at[batch, cols, to],
            dst_ref=dst.at[batch, cols, a],
            send_sem=ssem.at[q],
            recv_sem=rsem.at[q],
            device_id=(to, b),
            device_id_type=MESH,
        )

    def all_blocks(q):
        batch, first, count = CHUNKS[q]
        cols = pl.ds(first, count)
        return pltpu.make_async_remote_copy(
            src_ref=src.at[batch, cols, pl.ds(0, NS - 1)],
            dst_ref=dst.at[batch, cols, pl.ds(0, NS - 1)],
            send_sem=ssem.at[q],
            recv_sem=rsem.at[q],
            device_id=partner,
            device_id_type=MESH,
        )

    def send(q, k):
        block_copy(q, peer(k)).start()

    def send_all(peers):
        for q in range(len(CHUNKS)):
            for k in peers:
                send(q, k)

    for k in Y_LINE + Z_LINE:
        tell(near_sem, k)
    send_all(LINES)
    pl.semaphore_wait(near_sem, len(Y_LINE + Z_LINE))
    for k in Z_LINE:
        tell(wide_sem, k)
    send_all(PLANES)
    own = [
        pltpu.make_async_copy(src.at[batch, :, a], dst.at[batch, :, a], lsem.at[batch])
        for batch in range(BATCHES)
    ]
    for copy in own:
        copy.start()

    tab[...] = jnp.full(tab.shape, -1.0, F32)
    for load in loads[2:]:
        load.wait()
    for side in range(2):
        pair, place, parity = (small[3 * side + i] for i in range(3))
        tab[2 * side, :, 0:EXC] = pair.astype(F32)
        tab[2 * side + 1, :, 0:EXC] = ((1 - 2 * parity) * (place + 1)).astype(F32)
    pair_lane = lax.broadcasted_iota(jnp.int32, (EPAD, PPAD), 1).astype(F32)
    for side in range(2):
        pair_cols = tab[2 * side].T[0:EPAD]
        code_cols = tab[2 * side + 1].T[0:EPAD]
        for row in range(NV):
            hit = pair_cols[:, row : row + 1] == pair_lane
            codes[side, row] = jnp.sum(
                jnp.where(hit, code_cols[:, row : row + 1], 0.0), axis=0, keepdims=True
            )

    def signed_hot(code, count):
        place = (lax.broadcasted_iota(jnp.int32, (count, PPAD), 0) + 1).astype(F32)
        return (jnp.where(code == place, 1.0, 0.0) - jnp.where(code == -place, 1.0, 0.0)).astype(
            BF16
        )

    def beta_row(v, carry):
        tscr[pl.ds(pl.multiple_of(v * NU, NU), NU), :] = signed_hot(codes[0, v], NU)
        return carry

    lax.fori_loop(0, NV, beta_row, 0)
    ipad[...] = jnp.zeros(ipad.shape, BF16)
    ipad[0:PAIRS, 0:PAIRS] = integrals[...]
    table = jnp.dot(tscr[...], ipad[...], preferred_element_type=F32)
    high = table.astype(BF16)
    wscr[:, 0:PPAD] = high
    wscr[:, PPAD:] = (table - high.astype(F32)).astype(BF16)

    pl.semaphore_wait(wide_sem, len(Z_LINE))
    send_all(REST)

    def alpha_rows(step):
        for i in range(GSTEP):
            hot = signed_hot(codes[1, step * GSTEP + i], SLOTS)
            hots[i * SLOTS : (i + 1) * SLOTS, 0:PPAD] = hot
            hots[i * SLOTS : (i + 1) * SLOTS, PPAD:] = hot
        product = lax.dot_general(
            wscr[...], hots[...], (((1,), (1,)), ((), ())), preferred_element_type=F32
        )
        batch = step // (GB // GSTEP)
        for i in range(GSTEP):
            local = step % (GB // GSTEP) * GSTEP + i
            value = product[:, i * SLOTS : (i + 1) * SLOTS]
            top = value.astype(BF16)
            rest = (value - top.astype(F32)).astype(BF16)
            for v in range(NV):
                rows = slice(v * NU, (v + 1) * NU)
                start = (v // 2) * 2 * SLOTS
                alhs[batch, v % 2, local, :, start : start + SLOTS] = top[rows]
                alhs[batch, v % 2, local, :, start + SLOTS : start + 2 * SLOTS] = rest[rows]

    for step in range(NG // GSTEP):
        alpha_rows(step)
    swaps, keeps = [], []
    for batch in range(BATCHES):
        for h in range(2):
            place = (pl.ds(batch * GB * SB, GB * SB), pl.ds(h * 128, 128))
            swaps.append(
                pltpu.make_async_remote_copy(
                    src_ref=part.at[batch, 1 - b, h],
                    dst_ref=far_ref.at[place],
                    send_sem=psem.at[batch, h],
                    recv_sem=qsem.at[batch, h],
                    device_id=partner,
                    device_id_type=MESH,
                )
            )
            keeps.append(
                pltpu.make_async_copy(part.at[batch, b, h], own_ref.at[place], ksem.at[batch, h])
            )
    small_group = lax.broadcasted_iota(jnp.int32, (GB, 128), 1) // 16
    for batch in range(BATCHES):
        own[batch].wait()
        for q, (of_batch, first, count) in enumerate(CHUNKS):
            if of_batch != batch:
                continue
            all_blocks(q).wait_recv()
            right = []
            for w in range(first, first + count):
                right += [dst[batch, w].reshape(SLOTS, 128)] * 2
            lanes = slice(first * 2 * SLOTS, (first + count) * 2 * SLOTS)
            left = alhs[batch, :, :, :, lanes].reshape(2 * GB * NU, count * 2 * SLOTS)
            result = jnp.dot(left, jnp.concatenate(right, axis=0), preferred_element_type=F32)
            if first > 0:
                result = result + fsum[...]
            if first + count < WCH:
                fsum[...] = result
        even, odd = result[0 : GB * NU], result[GB * NU :]
        xscr[...] = even + pltpu.roll(odd, 64, 1)
        for j in range(4):
            by_u = [xscr[pl.ds(8 * j + i, GB, stride=NU), :] for i in range(8)]
            total = [jnp.zeros((GB, 128), F32) for _ in range(SB)]
            for d in range(8):
                mixed = by_u[d % 8]
                for s in range(1, SB):
                    mixed = jnp.where(small_group == s, by_u[(s + d) % 8], mixed)
                moved = pltpu.roll(mixed, 16 * d, 1) if d else mixed
                for s in range(SB):
                    total[s] = jnp.where(small_group == (s + d) % 8, moved, total[s])
            for s in range(SB):
                part.at[batch, j // 2, j % 2][pl.ds(s, GB, stride=SB), :] = total[s]
        for h in range(2):
            swaps[2 * batch + h].start()
            keeps[2 * batch + h].start()

    for q in range(len(CHUNKS)):
        all_blocks(q).wait_send()
    for swap, keep in zip(swaps, keeps):
        keep.wait()
        swap.wait()


def on_device(*operands):
    whole = pl.BlockSpec(memory_space=pl.ANY)
    own, far = pl.pallas_call(
        kernel,
        out_shape=[jax.ShapeDtypeStruct((64, 256), F32)] * 2,
        in_specs=[whole] * 9,
        out_specs=[whole] * 2,
        scratch_shapes=[
            pltpu.VMEM((64, 256), BF16),
            pltpu.VMEM((PAIRS, PAIRS), BF16),
            pltpu.VMEM((1, BATCHES * SLOTS), jnp.int32),
            pltpu.VMEM((6, 16, EXC), jnp.int32),
            pltpu.VMEM((2, 64, 128), F32),
            pltpu.VMEM((BATCHES, WCH, NS, CAP, 128), BF16),
            pltpu.VMEM((BATCHES, WCH, NS, CAP, 128), BF16),
            pltpu.VMEM((4, 16, 256), F32),
            pltpu.VMEM((2, NV, 1, PPAD), F32),
            pltpu.VMEM((NV * NU, PPAD), BF16),
            pltpu.VMEM((PPAD, PPAD), BF16),
            pltpu.VMEM((NV * NU, 2 * PPAD), BF16),
            pltpu.VMEM((BATCHES, 2, GB, NU, WCH * 2 * SLOTS), BF16),
            pltpu.VMEM((GSTEP * SLOTS, 2 * PPAD), BF16),
            pltpu.VMEM((2 * GB * NU, 128), F32),
            pltpu.VMEM((GB * NU, 128), F32),
            pltpu.VMEM((BATCHES, 2, 2, GB * SB, 128), F32),
            pltpu.SemaphoreType.REGULAR,
            pltpu.SemaphoreType.REGULAR,
            pltpu.SemaphoreType.DMA((9,)),
            pltpu.SemaphoreType.DMA((len(CHUNKS),)),
            pltpu.SemaphoreType.DMA((len(CHUNKS),)),
            pltpu.SemaphoreType.DMA((BATCHES,)),
            pltpu.SemaphoreType.DMA((BATCHES, 2)),
            pltpu.SemaphoreType.DMA((BATCHES, 2)),
            pltpu.SemaphoreType.DMA((BATCHES, 2)),
        ],
        compiler_params=pltpu.CompilerParams(
            collective_id=0, has_side_effects=True, vmem_limit_bytes=56 << 20
        ),
    )(*operands)
    return own + far


def solution(mesh):
    in_specs = (
        P("alpha", "beta"),
        P(),
        P("alpha", None),
        P("alpha", None),
        P("alpha", None),
        P("alpha", None),
        P("beta", None),
        P("beta", None),
        P("beta", None),
    )
    return jax.shard_map(
        on_device, mesh=mesh, in_specs=in_specs, out_specs=P("alpha", "beta"), check_vma=False
    )
```

time: 33.4 us -> 30 us (0.90)
  Pallas kernels: 31.7 us -> 28.3 us
  other arithmetic: 0 us -> 1.51 us
  local copies, waits for them, and re-layouts: 1.47 us -> 0 us
    pallas_call x1, Pallas kernels: 31.7 us -> 28.3 us  [on_device(): pl.pallas_call(kernel, out_shape=[jax.ShapeDtypeStruct((64, 256), F32)] *...]
    add x0 -> x1, other arithmetic: none -> 1.51 us  [on_device(): return own + far]
    unnamed x1 -> x0, local copies, waits for them, and re-layouts: 1.47 us -> none
where the time goes in v2:
time: 30 us; the launch traced here: 29.8 us
  Pallas kernels  28.3 us (94%)
  other arithmetic  1.51 us (5%)
    pallas_call x1, Pallas kernels, on_device(): pl.pallas_call(kernel, out_shape=[jax.ShapeDtypeStruct((64, 256), F32)] *...  28.3 us
    add x1, other arithmetic, on_device(): return own + far  1.51 us

profile of v2, /device:TPU:1, one launch (start us, length us, event | category | flops | bytes accessed | tf_op | source)
XLA Modules:
  0.0 29.8 jit_solution(3134178201485637897)
XLA Ops:
  0.0 28.3 %shard_map.91 = (f32[64,256]{1,0:T(8,128)}, f32[64,256]{1,0:T(8,128)}) custom-call(bf16[64,256]{1,0:T(8,128)(2,1)} %coeffs_ref.1, bf16[484,484]{1,0:T(8,128)(2,1)} %integrals_ref.1, s32[1,512]{1,0:T(1,128)} %send_ref.1, s32[16,132]{1,0:T(8,128)} %aslot_ref.1, s32[16,132]{1,0:T(8,128)} %apair_ref.1, s32[16,132]{1,0:T(8,128)} %apar_ref.1, ...), custom_call_target="tpu_custom_call" | custom-call | tf_op jit(solution)/shard_map/pallas_call | solution.py:310
  28.3 1.5 %add.3 = f32[64,256]{1,0:T(8,128)} add(f32[64,256]{1,0:T(8,128)} %get-tuple-element.7, f32[64,256]{1,0:T(8,128)} %get-tuple-element.8) | non-fusion elementwise | flops 16384 | bytes 196608 | tf_op jit(solution)/shard_map/add | solution.py:347

commit v3 on v2

--- a/solution.py
+++ b/solution.py
@@ -30,10 +30,21 @@
 
 PLANES = tuple(k for k in range(1, 64) if dims_of(k) == 2)
 REST = tuple(k for k in range(1, 64) if dims_of(k) == 3)
-CHUNKS = ((0, 0, 8), (1, 0, 4), (1, 4, 4))
+NEAR = LINES + PLANES
+ORDER = (0,) + LINES + PLANES[:22] + REST + PLANES[22:]
+POS = tuple(ORDER.index(k) for k in range(64))
+CHUNKS = (
+    (NEAR, 0, 0, 8),
+    (NEAR, 1, 0, 8),
+    (REST, 0, 0, 8),
+    (REST, 1, 0, 4),
+    (REST, 1, 4, 4),
+)
+STEPS = ((0, 0, 0), (1, 0, 1), (0, 1, 2), (1, 1, 3), (1, 1, 4))
 WCH = 8
 SLOTS = NS * CAP
 GSTEP = 4
+HALF = SLOTS // 2
 F32 = jnp.float32
 BF16 = jnp.bfloat16
 
@@ -140,12 +151,12 @@
 
     pl.semaphore_wait(barrier, len(LINES) + 1)
 
-    def block_copy(q, to):
-        batch, first, count = CHUNKS[q]
-        cols = pl.ds(first, count)
+    def block_copy(q, k):
+        _, batch, first, count = CHUNKS[q]
+        cols, to = pl.ds(first, count), peer(k)
         return pltpu.make_async_remote_copy(
             src_ref=src.at[batch, cols, to],
-            dst_ref=dst.at[batch, cols, a],
+            dst_ref=dst.at[batch, cols, POS[k]],
             send_sem=ssem.at[q],
             recv_sem=rsem.at[q],
             device_id=(to, b),
@@ -153,11 +164,11 @@
         )
 
     def all_blocks(q):
-        batch, first, count = CHUNKS[q]
+        peers, batch, first, count = CHUNKS[q]
         cols = pl.ds(first, count)
         return pltpu.make_async_remote_copy(
-            src_ref=src.at[batch, cols, pl.ds(0, NS - 1)],
-            dst_ref=dst.at[batch, cols, pl.ds(0, NS - 1)],
+            src_ref=src.at[batch, cols, pl.ds(0, len(peers))],
+            dst_ref=dst.at[batch, cols, pl.ds(0, len(peers))],
             send_sem=ssem.at[q],
             recv_sem=rsem.at[q],
             device_id=partner,
@@ -165,12 +176,13 @@
         )
 
     def send(q, k):
-        block_copy(q, peer(k)).start()
+        block_copy(q, k).start()
 
     def send_all(peers):
-        for q in range(len(CHUNKS)):
+        for q, chunk in enumerate(CHUNKS):
             for k in peers:
-                send(q, k)
+                if k in chunk[0]:
+                    send(q, k)
 
     for k in Y_LINE + Z_LINE:
         tell(near_sem, k)
@@ -180,7 +192,7 @@
         tell(wide_sem, k)
     send_all(PLANES)
     own = [
-        pltpu.make_async_copy(src.at[batch, :, a], dst.at[batch, :, a], lsem.at[batch])
+        pltpu.make_async_copy(src.at[batch, :, a], dst.at[batch, :, POS[0]], lsem.at[batch])
         for batch in range(BATCHES)
     ]
     for copy in own:
@@ -191,6 +203,17 @@
         load.wait()
     for side in range(2):
         pair, place, parity = (small[3 * side + i] for i in range(3))
+        if side == 1:
+            sender = lax.shift_right_logical(place, 2)
+            apart = (
+                ((here[0] - lax.shift_right_logical(sender, 4)) & 3) * 16
+                + ((here[1] - (lax.shift_right_logical(sender, 2) & 3)) & 3) * 4
+                + ((here[2] - (sender & 3)) & 3)
+            )
+            slot = place & 3
+            for k in range(NS):
+                slot = slot + jnp.where(apart == k, POS[k] * CAP, 0)
+            place = slot
         tab[2 * side, :, 0:EXC] = pair.astype(F32)
         tab[2 * side + 1, :, 0:EXC] = ((1 - 2 * parity) * (place + 1)).astype(F32)
     pair_lane = lax.broadcasted_iota(jnp.int32, (EPAD, PPAD), 1).astype(F32)
@@ -240,9 +263,11 @@
             rest = (value - top.astype(F32)).astype(BF16)
             for v in range(NV):
                 rows = slice(v * NU, (v + 1) * NU)
-                start = (v // 2) * 2 * SLOTS
-                alhs[batch, v % 2, local, :, start : start + SLOTS] = top[rows]
-                alhs[batch, v % 2, local, :, start + SLOTS : start + 2 * SLOTS] = rest[rows]
+                for half in range(2):
+                    start = half * WCH * SLOTS + (v // 2) * SLOTS
+                    lanes = slice(half * HALF, (half + 1) * HALF)
+                    alhs[batch, v % 2, local, :, start : start + HALF] = top[rows, lanes]
+                    alhs[batch, v % 2, local, :, start + HALF : start + SLOTS] = rest[rows, lanes]
 
     for step in range(NG // GSTEP):
         alpha_rows(step)
@@ -264,22 +289,26 @@
                 pltpu.make_async_copy(part.at[batch, b, h], own_ref.at[place], ksem.at[batch, h])
             )
     small_group = lax.broadcasted_iota(jnp.int32, (GB, 128), 1) // 16
-    for batch in range(BATCHES):
-        own[batch].wait()
-        for q, (of_batch, first, count) in enumerate(CHUNKS):
-            if of_batch != batch:
-                continue
-            all_blocks(q).wait_recv()
-            right = []
-            for w in range(first, first + count):
-                right += [dst[batch, w].reshape(SLOTS, 128)] * 2
-            lanes = slice(first * 2 * SLOTS, (first + count) * 2 * SLOTS)
-            left = alhs[batch, :, :, :, lanes].reshape(2 * GB * NU, count * 2 * SLOTS)
-            result = jnp.dot(left, jnp.concatenate(right, axis=0), preferred_element_type=F32)
-            if first > 0:
-                result = result + fsum[...]
-            if first + count < WCH:
-                fsum[...] = result
+    for batch, half, q in STEPS:
+        _, _, first, count = CHUNKS[q]
+        if half == 0:
+            own[batch].wait()
+        all_blocks(q).wait_recv()
+        right = []
+        for w in range(first, first + count):
+            right += [dst[batch, w, half * NS // 2 : (half + 1) * NS // 2].reshape(HALF, 128)] * 2
+        start = half * WCH * SLOTS + first * SLOTS
+        left = alhs[batch, :, :, :, start : start + count * SLOTS]
+        result = jnp.dot(
+            left.reshape(2 * GB * NU, count * SLOTS),
+            jnp.concatenate(right, axis=0),
+            preferred_element_type=F32,
+        )
+        if half == 1:
+            result = result + fsum[batch]
+        if half == 0 or first + count < WCH:
+            fsum[batch] = result
+            continue
         even, odd = result[0 : GB * NU], result[GB * NU :]
         xscr[...] = even + pltpu.roll(odd, 64, 1)
         for j in range(4):
@@ -310,8 +339,8 @@
     own, far = pl.pallas_call(
         kernel,
         out_shape=[jax.ShapeDtypeStruct((64, 256), F32)] * 2,
-        in_specs=[whole] * 9,
-        out_specs=[whole] * 2,
+        in_specs=[pl.BlockSpec(memory_space=pltpu.HBM)] * 9,
+        out_specs=[pl.BlockSpec(memory_space=pltpu.VMEM)] * 2,
         scratch_shapes=[
             pltpu.VMEM((64, 256), BF16),
             pltpu.VMEM((PAIRS, PAIRS), BF16),
@@ -327,7 +356,7 @@
             pltpu.VMEM((NV * NU, 2 * PPAD), BF16),
             pltpu.VMEM((BATCHES, 2, GB, NU, WCH * 2 * SLOTS), BF16),
             pltpu.VMEM((GSTEP * SLOTS, 2 * PPAD), BF16),
-            pltpu.VMEM((2 * GB * NU, 128), F32),
+            pltpu.VMEM((BATCHES, 2 * GB * NU, 128), F32),
             pltpu.VMEM((GB * NU, 128), F32),
             pltpu.VMEM((BATCHES, 2, 2, GB * SB, 128), F32),
             pltpu.SemaphoreType.REGULAR,
@@ -341,9 +370,9 @@
             pltpu.SemaphoreType.DMA((BATCHES, 2)),
         ],
         compiler_params=pltpu.CompilerParams(
-            collective_id=0, has_side_effects=True, vmem_limit_bytes=56 << 20
+            collective_id=0, has_side_effects=True, vmem_limit_bytes=28 << 20
         ),
-    )(*operands)
+    )(*[pltpu.with_memory_space_constraint(x, pltpu.HBM) for x in operands])
     return own + far
 
 

time: 30 us -> 27.2 us (0.907)
  Pallas kernels: 28.3 us -> 26.5 us
  other arithmetic: 1.51 us -> 0.64 us
    pallas_call x1, Pallas kernels: 28.3 us -> 26.5 us  [on_device(): pl.pallas_call(kernel, out_shape=[jax.ShapeDtypeStruct((64, 256), F32)] *...]
    add x1, other arithmetic: 1.51 us -> 0.64 us  [on_device(): return own + far]
where the time goes in v3:
time: 27.2 us; the launch traced here: 27.1 us
  Pallas kernels  26.5 us (97%)
  other arithmetic  0.64 us (2%)
    pallas_call x1, Pallas kernels, on_device(): pl.pallas_call(kernel, out_shape=[jax.ShapeDtypeStruct((64, 256), F32)] *...  26.5 us
    add x1, other arithmetic, on_device(): return own + far  0.64 us

profile of v3, /device:TPU:1, one launch (start us, length us, event | category | flops | bytes accessed | tf_op | source)
XLA Modules:
  0.0 27.1 jit_solution(3250514071450583354)
XLA Ops:
  0.0 26.5 %shard_map.91 = (f32[64,256]{1,0:T(8,128)S(1)}, f32[64,256]{1,0:T(8,128)S(1)}) custom-call(bf16[64,256]{1,0:T(8,128)(2,1)} %coeffs_ref.1, bf16[484,484]{1,0:T(8,128)(2,1)} %integrals_ref.1, s32[1,512]{1,0:T(1,128)} %send_ref.1, s32[16,132]{1,0:T(8,128)} %aslot_ref.1, s32[16,132]{1,0:T(8,128)} %apair_ref.1, s32[16,132]{1,0:T(8,128)} %apar_ref.1, ...), custom_call_target="tpu_custom_call" | custom-call | tf_op jit(solution)/shard_map/pallas_call | solution.py:339
  26.5 0.6 %add.3 = f32[64,256]{1,0:T(8,128)} add(f32[64,256]{1,0:T(8,128)S(1)} %get-tuple-element.7, f32[64,256]{1,0:T(8,128)S(1)} %get-tuple-element.8) | non-fusion elementwise | flops 16384 | bytes 196608 | tf_op jit(solution)/shard_map/add | solution.py:376

commit v4 on v3

--- a/solution.py
+++ b/solution.py
@@ -31,6 +31,13 @@
 PLANES = tuple(k for k in range(1, 64) if dims_of(k) == 2)
 REST = tuple(k for k in range(1, 64) if dims_of(k) == 3)
 NEAR = LINES + PLANES
+
+
+def first_leg(k):
+    digits = (k % 4, k // 4 % 4 * 4, k // 16 * 16)
+    return digits[sum((k % 4, k // 4 % 4, k // 16)) % 3]
+
+
 ORDER = (0,) + LINES + PLANES[:22] + REST + PLANES[22:]
 POS = tuple(ORDER.index(k) for k in range(64))
 CHUNKS = (
@@ -74,12 +81,14 @@
     ipad,
     wscr,
     alhs,
+    transit,
     hots,
     fsum,
     xscr,
     part,
     near_sem,
-    wide_sem,
+    tsend,
+    trecv,
     insem,
     ssem,
     rsem,
@@ -151,6 +160,39 @@
 
     pl.semaphore_wait(barrier, len(LINES) + 1)
 
+    def first_copy(batch, i):
+        to, relay = peer(REST[i]), peer(first_leg(REST[i]))
+        return pltpu.make_async_remote_copy(
+            src_ref=src.at[batch, :, to],
+            dst_ref=transit.at[batch, :, i],
+            send_sem=tsend.at[batch],
+            recv_sem=trecv.at[batch],
+            device_id=(relay, b),
+            device_id_type=MESH,
+        )
+
+    def in_transit(batch):
+        return pltpu.make_async_remote_copy(
+            src_ref=src.at[batch, :, pl.ds(0, len(REST))],
+            dst_ref=transit.at[batch],
+            send_sem=tsend.at[batch],
+            recv_sem=trecv.at[batch],
+            device_id=partner,
+            device_id_type=MESH,
+        )
+
+    def forward(q, i):
+        _, batch, first, count = CHUNKS[q]
+        cols, k = pl.ds(first, count), REST[i]
+        return pltpu.make_async_remote_copy(
+            src_ref=transit.at[batch, cols, i],
+            dst_ref=dst.at[batch, cols, POS[k]],
+            send_sem=ssem.at[q],
+            recv_sem=rsem.at[q],
+            device_id=(peer(k - first_leg(k)), b),
+            device_id_type=MESH,
+        )
+
     def block_copy(q, k):
         _, batch, first, count = CHUNKS[q]
         cols, to = pl.ds(first, count), peer(k)
@@ -186,11 +228,10 @@
 
     for k in Y_LINE + Z_LINE:
         tell(near_sem, k)
+    for batch in range(BATCHES):
+        for i in range(len(REST)):
+            first_copy(batch, i).start()
     send_all(LINES)
-    pl.semaphore_wait(near_sem, len(Y_LINE + Z_LINE))
-    for k in Z_LINE:
-        tell(wide_sem, k)
-    send_all(PLANES)
     own = [
         pltpu.make_async_copy(src.at[batch, :, a], dst.at[batch, :, POS[0]], lsem.at[batch])
         for batch in range(BATCHES)
@@ -244,8 +285,14 @@
     wscr[:, 0:PPAD] = high
     wscr[:, PPAD:] = (table - high.astype(F32)).astype(BF16)
 
-    pl.semaphore_wait(wide_sem, len(Z_LINE))
-    send_all(REST)
+    pl.semaphore_wait(near_sem, len(Y_LINE + Z_LINE))
+    send_all(PLANES)
+    for batch in range(BATCHES):
+        in_transit(batch).wait_recv()
+        for q, chunk in enumerate(CHUNKS):
+            if chunk[0] == REST and chunk[1] == batch:
+                for i in range(len(REST)):
+                    forward(q, i).start()
 
     def alpha_rows(step):
         for i in range(GSTEP):
@@ -327,6 +374,8 @@
             swaps[2 * batch + h].start()
             keeps[2 * batch + h].start()
 
+    for batch in range(BATCHES):
+        in_transit(batch).wait_send()
     for q in range(len(CHUNKS)):
         all_blocks(q).wait_send()
     for swap, keep in zip(swaps, keeps):
@@ -355,12 +404,14 @@
             pltpu.VMEM((PPAD, PPAD), BF16),
             pltpu.VMEM((NV * NU, 2 * PPAD), BF16),
             pltpu.VMEM((BATCHES, 2, GB, NU, WCH * 2 * SLOTS), BF16),
+            pltpu.VMEM((BATCHES, WCH, len(REST), CAP, 128), BF16),
             pltpu.VMEM((GSTEP * SLOTS, 2 * PPAD), BF16),
             pltpu.VMEM((BATCHES, 2 * GB * NU, 128), F32),
             pltpu.VMEM((GB * NU, 128), F32),
             pltpu.VMEM((BATCHES, 2, 2, GB * SB, 128), F32),
             pltpu.SemaphoreType.REGULAR,
-            pltpu.SemaphoreType.REGULAR,
+            pltpu.SemaphoreType.DMA((BATCHES,)),
+            pltpu.SemaphoreType.DMA((BATCHES,)),
             pltpu.SemaphoreType.DMA((9,)),
             pltpu.SemaphoreType.DMA((len(CHUNKS),)),
             pltpu.SemaphoreType.DMA((len(CHUNKS),)),

time: 27.2 us -> 26.3 us (0.967)
  Pallas kernels: 26.5 us -> 25.5 us
    pallas_call x1, Pallas kernels: 26.5 us -> 25.5 us  [on_device(): pl.pallas_call(kernel, out_shape=[jax.ShapeDtypeStruct((64, 256), F32)] *...]
where the time goes in v4:
time: 26.3 us; the launch traced here: 26.2 us
  Pallas kernels  25.5 us (97%)
  other arithmetic  0.64 us (2%)
    pallas_call x1, Pallas kernels, on_device(): pl.pallas_call(kernel, out_shape=[jax.ShapeDtypeStruct((64, 256), F32)] *...  25.5 us
    add x1, other arithmetic, on_device(): return own + far  0.64 us

profile of v4, /device:TPU:1, one launch (start us, length us, event | category | flops | bytes accessed | tf_op | source)
XLA Modules:
  0.0 26.2 jit_solution(13186222400052110804)
XLA Ops:
  0.0 25.5 %shard_map.91 = (f32[64,256]{1,0:T(8,128)S(1)}, f32[64,256]{1,0:T(8,128)S(1)}) custom-call(bf16[64,256]{1,0:T(8,128)(2,1)} %coeffs_ref.1, bf16[484,484]{1,0:T(8,128)(2,1)} %integrals_ref.1, s32[1,512]{1,0:T(1,128)} %send_ref.1, s32[16,132]{1,0:T(8,128)} %aslot_ref.1, s32[16,132]{1,0:T(8,128)} %apair_ref.1, s32[16,132]{1,0:T(8,128)} %apar_ref.1, ...), custom_call_target="tpu_custom_call" | custom-call | tf_op jit(solution)/shard_map/pallas_call | solution.py:388
  25.6 0.6 %add.3 = f32[64,256]{1,0:T(8,128)} add(f32[64,256]{1,0:T(8,128)S(1)} %get-tuple-element.7, f32[64,256]{1,0:T(8,128)S(1)} %get-tuple-element.8) | non-fusion elementwise | flops 16384 | bytes 196608 | tf_op jit(solution)/shard_map/add | solution.py:427

commit v5 on v4

--- a/solution.py
+++ b/solution.py
@@ -47,7 +47,7 @@
     (REST, 1, 0, 4),
     (REST, 1, 4, 4),
 )
-STEPS = ((0, 0, 0), (1, 0, 1), (0, 1, 2), (1, 1, 3), (1, 1, 4))
+STEPS = ((0, 0, 0), (0, 1, 2), (1, 0, 1), (1, 1, 3), (1, 1, 4))
 WCH = 8
 SLOTS = NS * CAP
 GSTEP = 4
@@ -286,8 +286,9 @@
     wscr[:, PPAD:] = (table - high.astype(F32)).astype(BF16)
 
     pl.semaphore_wait(near_sem, len(Y_LINE + Z_LINE))
-    send_all(PLANES)
     for batch in range(BATCHES):
+        for k in PLANES:
+            send(batch, k)
         in_transit(batch).wait_recv()
         for q, chunk in enumerate(CHUNKS):
             if chunk[0] == REST and chunk[1] == batch:

time: 26.3 us -> 25.9 us (0.985)
  Pallas kernels: 25.5 us -> 25.1 us
    pallas_call x1, Pallas kernels: 25.5 us -> 25.1 us  [on_device(): pl.pallas_call(kernel, out_shape=[jax.ShapeDtypeStruct((64, 256), F32)] *...]
where the time goes in v5:
time: 25.9 us; the launch traced here: 25.8 us
  Pallas kernels  25.1 us (97%)
  other arithmetic  0.64 us (2%)
    pallas_call x1, Pallas kernels, on_device(): pl.pallas_call(kernel, out_shape=[jax.ShapeDtypeStruct((64, 256), F32)] *...  25.1 us
    add x1, other arithmetic, on_device(): return own + far  0.64 us

profile of v5, /device:TPU:1, one launch (start us, length us, event | category | flops | bytes accessed | tf_op | source)
XLA Modules:
  0.0 25.8 jit_solution(10420225376224472047)
XLA Ops:
  0.0 25.1 %shard_map.91 = (f32[64,256]{1,0:T(8,128)S(1)}, f32[64,256]{1,0:T(8,128)S(1)}) custom-call(bf16[64,256]{1,0:T(8,128)(2,1)} %coeffs_ref.1, bf16[484,484]{1,0:T(8,128)(2,1)} %integrals_ref.1, s32[1,512]{1,0:T(1,128)} %send_ref.1, s32[16,132]{1,0:T(8,128)} %aslot_ref.1, s32[16,132]{1,0:T(8,128)} %apair_ref.1, s32[16,132]{1,0:T(8,128)} %apar_ref.1, ...), custom_call_target="tpu_custom_call" | custom-call | tf_op jit(solution)/shard_map/pallas_call | solution.py:389
  25.1 0.6 %add.3 = f32[64,256]{1,0:T(8,128)} add(f32[64,256]{1,0:T(8,128)S(1)} %get-tuple-element.7, f32[64,256]{1,0:T(8,128)S(1)} %get-tuple-element.8) | non-fusion elementwise | flops 16384 | bytes 196608 | tf_op jit(solution)/shard_map/add | solution.py:428

commit v6 on v5

--- a/solution.py
+++ b/solution.py
@@ -285,16 +285,6 @@
     wscr[:, 0:PPAD] = high
     wscr[:, PPAD:] = (table - high.astype(F32)).astype(BF16)
 
-    pl.semaphore_wait(near_sem, len(Y_LINE + Z_LINE))
-    for batch in range(BATCHES):
-        for k in PLANES:
-            send(batch, k)
-        in_transit(batch).wait_recv()
-        for q, chunk in enumerate(CHUNKS):
-            if chunk[0] == REST and chunk[1] == batch:
-                for i in range(len(REST)):
-                    forward(q, i).start()
-
     def alpha_rows(step):
         for i in range(GSTEP):
             hot = signed_hot(codes[1, step * GSTEP + i], SLOTS)
@@ -317,7 +307,19 @@
                     alhs[batch, v % 2, local, :, start : start + HALF] = top[rows, lanes]
                     alhs[batch, v % 2, local, :, start + HALF : start + SLOTS] = rest[rows, lanes]
 
-    for step in range(NG // GSTEP):
+    pl.semaphore_wait(near_sem, len(Y_LINE + Z_LINE))
+    for batch in range(BATCHES):
+        for k in PLANES:
+            send(batch, k)
+        if batch == 0:
+            alpha_rows(0)
+        in_transit(batch).wait_recv()
+        for q, chunk in enumerate(CHUNKS):
+            if chunk[0] == REST and chunk[1] == batch:
+                for i in range(len(REST)):
+                    forward(q, i).start()
+
+    for step in range(1, NG // GSTEP):
         alpha_rows(step)
     swaps, keeps = [], []
     for batch in range(BATCHES):

time: 25.9 us -> 25.9 us (level)
  no operation moved by 1% of the time
where the time goes in v6:
time: 25.9 us; the launch traced here: 25.8 us
  Pallas kernels  25.1 us (97%)
  other arithmetic  0.64 us (2%)
    pallas_call x1, Pallas kernels, on_device(): pl.pallas_call(kernel, out_shape=[jax.ShapeDtypeStruct((64, 256), F32)] *...  25.1 us
    add x1, other arithmetic, on_device(): return own + far  0.64 us

profile of v6, /device:TPU:1, one launch (start us, length us, event | category | flops | bytes accessed | tf_op | source)
XLA Modules:
  0.0 25.8 jit_solution(4584969195740118968)
XLA Ops:
  0.0 25.1 %shard_map.91 = (f32[64,256]{1,0:T(8,128)S(1)}, f32[64,256]{1,0:T(8,128)S(1)}) custom-call(bf16[64,256]{1,0:T(8,128)(2,1)} %coeffs_ref.1, bf16[484,484]{1,0:T(8,128)(2,1)} %integrals_ref.1, s32[1,512]{1,0:T(1,128)} %send_ref.1, s32[16,132]{1,0:T(8,128)} %aslot_ref.1, s32[16,132]{1,0:T(8,128)} %apair_ref.1, s32[16,132]{1,0:T(8,128)} %apar_ref.1, ...), custom_call_target="tpu_custom_call" | custom-call | tf_op jit(solution)/shard_map/pallas_call | solution.py:391
  25.1 0.6 %add.3 = f32[64,256]{1,0:T(8,128)} add(f32[64,256]{1,0:T(8,128)S(1)} %get-tuple-element.7, f32[64,256]{1,0:T(8,128)S(1)} %get-tuple-element.8) | non-fusion elementwise | flops 16384 | bytes 196608 | tf_op jit(solution)/shard_map/add | solution.py:430
